TPU v7x, 512 devices: a whole 4x4x16 slice. The times are simulated.
512 devices in a mesh: dp: 128 (over z, y, core), mp: 4 (over x).
Axes of the slice: x: 4, y: 4, z: 16, core: 2. Of those that a mesh axis runs over, the one named last changes fastest.
Arguments:
- queries: bfloat16 [65536, 4096], P('dp', 'mp'), may hold values from -150 to 150, as said below
- keys: bfloat16 [65536, 4096], P('dp', 'mp'), may hold values from -8 to 8
- values: bfloat16 [65536, 4096], P('dp', 'mp'), may hold values from -6 to 6
- out_weight: bfloat16 [4096, 2048], P('mp', 'dp'), may hold values from -0.375 to 0.375
- span_start: int32 [128], P('dp'), may hold values from 1 to 3
- span_len: int32 [128], P('dp'), may hold values from 1 to 3
Outputs:
- projected: bfloat16 [65536, 2048], P('dp', 'mp')
Inputs may be any that keep to these rules, and one draw needn't show every extreme that they name: `queries`: without the hidden law's aligned rows, entries are standard normal values clipped to 8 in magnitude.
All inputs are finite; a program needn't handle non-finite values.
Results may differ from a plain program's by a relative error of at most 0.0068.
Values may be sent and summed in bfloat16 or wider, within the bound.
A program may use at most 64 MiB of HBM per device.

v0:
```python
import jax
import jax.numpy as jnp
from jax import lax
from jax.sharding import Mesh
from jax.sharding import PartitionSpec as P

HD = 128
BLK = 128
DP = ("dp_0", "dp_1", "dp_2")


def joined_along(parts, dim):
    shape = list(parts.shape[1:])
    shape[dim] *= parts.shape[0]
    return jnp.moveaxis(parts, 0, dim).reshape(shape)


def stacked_from(value, axes, turns):
    parts = value
    for k in turns:
        parts = lax.all_gather(parts, axes[k])
    done = turns[::-1]
    back = [done.index(k) for k in range(len(axes))]
    parts = parts.transpose(*back, *range(len(axes), parts.ndim))
    return parts.reshape(-1, *value.shape)


def whole_of(value, axes, turns, dim):
    return joined_along(stacked_from(value, axes, turns), dim)


def cut_along(value, dim, size):
    before, after = (value.shape[:dim], value.shape[dim + 1 :])
    return jnp.moveaxis(value.reshape(*before, size, -1, *after), dim, 0)


def sent_and_summed(value, axis, dim):
    size = lax.axis_size(axis)
    parts = lax.all_to_all(cut_along(value, dim, size), axis, 0, 0, tiled=True)
    return jnp.sum(parts.astype(jnp.float32), axis=0)


def attend_local(query_rows, key_rows, value_rows, start, length):
    rows = query_rows.shape[0]
    heads_here = query_rows.shape[1] // HD
    position = jnp.arange(rows, dtype=jnp.int32)
    block = position // BLK
    finish = jnp.minimum(start + length, rows // BLK)
    image = (block >= start) & (block < finish)
    causal = position[None, :] <= position[:, None]
    allowed = jnp.where(image[:, None], image[None, :], causal)
    query_h = query_rows.reshape(rows, heads_here, HD)
    key_h = key_rows.reshape(rows, heads_here, HD)
    value_h = value_rows.reshape(rows, heads_here, HD)
    scores = jnp.einsum("qhd,khd->hqk", query_h, key_h, preferred_element_type=jnp.float32)
    scores = scores / jnp.sqrt(jnp.float32(HD))
    scores = jnp.where(allowed[None, :, :], scores, jnp.float32(-1e30))
    top = jnp.max(scores, axis=-1, keepdims=True)
    expo = jnp.exp(scores - top)
    weights = (expo / jnp.sum(expo, axis=-1, keepdims=True)).astype(jnp.bfloat16)
    result = jnp.einsum("hqk,khd->qhd", weights, value_h, preferred_element_type=jnp.float32)
    return result.astype(jnp.bfloat16).reshape(rows, heads_here * HD)


def shards(queries, keys, values, out_weight, span_start, span_len):
    attended = attend_local(queries, keys, values, span_start[0], span_len[0])
    full_weight = whole_of(out_weight, DP, (1, 0, 2), 1)
    partial_sums = jnp.dot(attended, full_weight, preferred_element_type=jnp.float32)
    summed = sent_and_summed(partial_sums.astype(jnp.bfloat16), "mp", 1)
    return summed.astype(jnp.bfloat16)


def solution(mesh):
    split = Mesh(mesh.devices.reshape(16, 4, 2, mesh.shape["mp"]), ("dp_0", "dp_1", "dp_2", "mp"))
    placed = (P(DP, "mp"), P(DP, "mp"), P(DP, "mp"), P("mp", DP), P(DP), P(DP))
    return jax.shard_map(
        shards, mesh=split, in_specs=placed, out_specs=P(DP, "mp"), check_vma=False
    )
```

profile of v0, /device:TPU:1, one launch (start us, length us, event | category | flops | bytes accessed | tf_op | source)
XLA Modules:
  0.0 164.0 jit_solution(13264346905037277779)
XLA Ops:
  6.5 0.0 copy-start
  6.5 0.0 all-gather.6.cloned.1.call-start
  6.5 10.8 %all-gather = bf16[4096,16]{0,1:T(8,128)(2,1)S(1)} all-gather(bf16[1024,16]{0,1:T(8,128)(2,1)} %param.9), channel_id=2, replica_groups=mesh['dp_0'=16,'dp_1'=4,'dp_2'=2,'mp'=4] {'dp_1'}, dimensions={0}, use_global_device_ids=true | all-gather | bytes 163840 | tf_op jit(solution)/shard_map/all_gather | solution.py:21
  17.3 0.7 copy.51
  18.0 0.0 all-gather.6.cloned.1.call-update
  18.0 0.0 all-gather.8.cloned.1.call-start
  18.1 70.2 %all-gather.6.cloned.1.call-done = bf16[64,1024,16]{1,2,0:T(8,128)(2,1)} async-done(((bf16[4,1024,16]{1,2,0:T(8,128)(2,1)}), bf16[64,1024,16]{1,2,0:T(8,128)(2,1)}) %all-gather.6.cloned.1.call-update) | async-done | bytes 2097168 | tf_op jit(solution)/shard_map/all_gather | solution.py:21
  88.2 0.0 all-gather.8.cloned.1.call-update
  89.6 1.5 copy.35
  91.1 0.2 fusion.12
  91.3 0.0 copy-done
  91.3 2.5 %fusion.7 = f32[8,512,512]{1,2,0:T(8,128)S(1)} fusion(bf16[512,1024]{1,0:T(8,128)(2,1)S(1)} %copy-done, bf16[512,1024]{1,0:T(8,128)(2,1)} %param.6), kind=kOutput, calls=%fused_computation.12 | convolution fusion | flops 536870912 | bytes 10485760 | tf_op jit(solution)/shard_map/qhd,khd->hqk/dot_general | solution.py:55
  93.8 5.7 %fusion.21 = (f32[8,512]{1,0:T(8,128)S(1)}, f32[8,512,512]{1,2,0:T(8,128)}) fusion(f32[8,512,512]{1,2,0:T(8,128)S(1)} %fusion.7, pred[512,512]{0,1:T(8,128)(4,1)S(1)} %fusion.12), kind=kOutput, calls=%fused_computation.32 | output fusion | flops 12583423 | bytes 17055744 | tf_op jit(solution)/shard_map/sub | solution.py:59
  99.5 4.1 %fusion.6 = bf16[8,512,128]{1,2,0:T(8,128)(2,1)S(1)} fusion(bf16[512,8,128]{0,2,1:T(8,128)(2,1)S(1)} %bitcast.51, f32[8,512,512]{1,2,0:T(8,128)} %get-tuple-element.6, f32[8,512]{1,0:T(8,128)S(1)} %get-tuple-element.5), kind=kOutput, calls=%fused_computation.11 | convolution fusion | flops 541589504 | bytes 10502144 | tf_op jit(solution)/shard_map/hqk,khd->qhd/dot_general | solution.py:61
  103.6 18.4 %all-gather.8.cloned.1.call-done = bf16[32,4,1024,16]{2,3,1,0:T(8,128)(2,1)} async-done(((bf16[16,4,1024,16]{2,3,1,0:T(8,128)(2,1)}), bf16[32,4,1024,16]{2,3,1,0:T(8,128)(2,1)}) %all-gather.8.cloned.1.call-update) | async-done | bytes 4194320 | tf_op jit(solution)/shard_map/all_gather | solution.py:21
  122.0 2.6 %copy.32 = bf16[16,4,2,1024,16]{3,4,2,1,0:T(8,128)(2,1)S(1)} copy(bf16[16,4,2,1024,16]{3,4,1,0,2:T(8,128)(2,1)} %bitcast.47) | data formatting | bytes 8388608 | tf_op jit(solution)/shard_map/transpose | solution.py:24
  124.7 2.4 %convolution_convert_fusion = bf16[512,2048]{1,0:T(8,128)(2,1)S(1)} fusion(bf16[512,1024]{0,1:T(8,128)(2,1)S(1)} %bitcast.54, bf16[1024,2048]{0,1:T(8,128)(2,1)S(1)} %bitcast.48), kind=kOutput, calls=%fused_computation.9 | convolution fusion | flops 2148532224 | bytes 7340032 | tf_op jit(solution)/shard_map/dot_general | solution.py:68
  127.1 0.2 copy.50
  127.2 28.7 %all_to_all.5 = bf16[4,512,512]{2,1,0:T(8,128)(2,1)S(1)} all-to-all(bf16[4,512,512]{2,1,0:T(8,128)(2,1)S(1)} %bitcast.46), channel_id=1, replica_groups=mesh['dp_0'=16,'dp_1'=4,'dp_2'=2,'mp'=4] {'mp'}, dimensions={0} | all-to-all | bytes 4194304 | tf_op jit(solution)/shard_map/all_to_all | solution.py:39
  155.9 1.2 reduce_sum.22
  (1 shorter events, 0.0 us)
Async XLA Ops:
  6.5 84.7 %copy-start = (bf16[512,1024]{1,0:T(8,128)(2,1)S(1)}, bf16[512,1024]{1,0:T(8,128)(2,1)}, u32[]{:S(2)}) copy-start(bf16[512,1024]{1,0:T(8,128)(2,1)} %param.7) | copy-start | bytes 3145732
  6.5 81.7 %all-gather.6.cloned.1.call-start = ((), (), s32[]{:S(2)}) async-start(), calls=%async_computation.1 | async-start | bytes 2228224 | tf_op jit(solution)/shard_map/all_gather | solution.py:21
  18.0 104.0 %all-gather.8.cloned.1.call-start = ((), (), s32[]{:S(2)}) async-start(), calls=%async_computation.2 | async-start | bytes 6291456 | tf_op jit(solution)/shard_map/all_gather | solution.py:21
Sparse Core Ops, SparseCore 0:
  18.1 70.0 all-gather.5
  90.3 31.6 all-gather.7
where the time goes:
time: 164 us
  waiting for transfers between devices  88.6 us (54%)
  blocking collectives  39.5 us (24%)
  between operations  14.8 us (9%)
  matrix products  8.99 us (5%)
  other arithmetic  7.13 us (4%)
  local copies, waits for them, and re-layouts  4.95 us (3%)
    all_gather x2, waiting for transfers between devices, stacked_from(): parts = lax.all_gather(parts, axes[k])  88.6 us
    all_to_all x1, blocking collectives, sent_and_summed(): parts = lax.all_to_all(cut_along(value, dim, size), axis, 0, 0, tiled=True)  28.7 us
    all_gather x1, blocking collectives, stacked_from(): parts = lax.all_gather(parts, axes[k])  10.8 us
    sub x1, other arithmetic, attend_local(): expo = jnp.exp(scores - top)  5.71 us
    dot_general x1, matrix products, attend_local(): jnp.einsum('hqk,khd->qhd', weights, value_h, preferred_element_type=jnp.f...  4.12 us
  transfers between devices with their start and end apart: 2, of which 2 were waited for; matrix products, arithmetic and copies ran while one was open for 9% of the time, Pallas kernels for 0%

commit v1 on v0

v1 whole, which is shorter than its diff:
```python
import functools

import jax
import jax.numpy as jnp
from jax import lax
from jax.experimental import pallas as pl
from jax.experimental.pallas import tpu as pltpu
from jax.sharding import PartitionSpec as P

MESH = pl.DeviceIdType.MESH
HD = 128
BLK = 128
SEQ = 512
HEADS = 8
FEAT = HEADS * HD
NEG = -1e30
SCALE = 1.4426950408889634 / (128.0**0.5)
TRANS = (((1,), (1,)), ((), ()))


def attend_head(q_ref, k_ref, v_ref, att, bias, h):
    cols = pl.ds(pl.multiple_of(h * HD, HD), HD)
    key = k_ref[:, cols]
    val = v_ref[:, cols]
    for qb in range(SEQ // BLK):
        rows = pl.ds(qb * BLK, BLK)
        keys = BLK if qb == 0 else SEQ
        s = lax.dot_general(q_ref[rows, cols], key[:keys], TRANS, preferred_element_type=jnp.float32)
        s = s + bias[rows, pl.ds(0, keys)]
        top = jnp.max(s, axis=-1, keepdims=True)
        p = jnp.exp2((s - top) * SCALE)
        total = jnp.sum(p, axis=-1, keepdims=True)
        o = jnp.dot(p.astype(jnp.bfloat16), val[:keys], preferred_element_type=jnp.float32)
        att[rows, cols] = (o / total).astype(jnp.bfloat16)


def kernel(start_ref, len_ref, q_hbm, k_hbm, v_hbm, w_hbm, o_ref,
           q, k, v, att, bias, wb, own, xs, xr,
           qsem, wsem, wr, wu, ws, fs, fr, xss, xrs):
    dp, x = lax.axis_index("dp"), lax.axis_index("mp")
    c = lax.rem(dp, 2)
    y = lax.rem(lax.div(dp, 2), 4)
    z = lax.div(dp, 8)
    a0, b0 = lax.div(z, 4), lax.rem(z, 4)
    two = 2 - 4 * lax.rem(z, 2)

    def at(dz=0, dy=0, dx=0, dc=0):
        zz, yy = lax.rem(z + dz + 16, 16), lax.rem(y + dy + 4, 4)
        return ((zz * 4 + yy) * 2 + lax.rem(c + dc, 2), lax.rem(x + dx + 4, 4))

    def group(dz):
        zz = lax.rem(z + dz + 16, 16)
        return lax.div(zz, 4), lax.rem(zz, 4)

    def turn(a, r):
        return lax.rem(a + r + 4, 4)

    barrier = pltpu.get_barrier_semaphore()
    partners = [at(dz=4), at(dz=-4), at(dz=8), at(dz=1), at(dz=-1), at(dz=2), at(dz=-2),
                at(dy=1), at(dy=-1), at(dy=2), at(dx=1), at(dx=2), at(dx=3), at(dc=1)]
    for who in partners:
        pl.semaphore_signal(barrier, inc=1, device_id=who, device_id_type=MESH)

    mine = wb.at[a0, b0, y, c]
    w_in = pltpu.make_async_copy(w_hbm, mine, wsem)
    w_in.start()

    def inputs(i):
        cols = pl.ds(pl.multiple_of(i * 256, 256), 256)
        return [pltpu.make_async_copy(src.at[:, cols], dst.at[:, cols], qsem.at[n, i])
                for n, (src, dst) in enumerate(((q_hbm, q), (k_hbm, k), (v_hbm, v)))]

    for i in range(4):
        for copy in inputs(i):
            copy.start()

    row = lax.broadcasted_iota(jnp.int32, (SEQ, SEQ), 0)
    col = lax.broadcasted_iota(jnp.int32, (SEQ, SEQ), 1)
    first = start_ref[0] * BLK
    last = jnp.minimum(start_ref[0] + len_ref[0], SEQ // BLK) * BLK
    image_row = (row >= first) & (row < last)
    image_col = (col >= first) & (col < last)
    bias[...] = jnp.where(image_row, jnp.where(image_col, 0.0, NEG), jnp.where(col <= row, 0.0, NEG))

    def heads(i, carry):
        for copy in inputs(i):
            copy.wait()
        for j in range(2):
            attend_head(q, k, v, att, bias, i * 2 + j)
        return carry

    lax.fori_loop(0, 2, heads, 0)

    sent = []

    def send(src, dst, sem, who):
        n = len(sent)
        copy = pltpu.make_async_remote_copy(src_ref=src, dst_ref=dst, send_sem=ws.at[n], recv_sem=sem,
                                            device_id=who, device_id_type=MESH)
        copy.start()
        sent.append(copy)

    def piece(a, b, yy, who):
        send(wb.at[a, b, yy, c], wb.at[a, b, yy, c], wr.at[a, b, yy], who)

    def got(ref, sem):
        pltpu.make_async_remote_copy(src_ref=ref, dst_ref=ref, send_sem=ws.at[0], recv_sem=sem,
                                     device_id=at(dc=1), device_id_type=MESH).wait_recv()

    def got_piece(a, b, yy):
        got(wb.at[a, b, yy, c], wr.at[a, b, yy])

    over_y = (1, -1, 2)

    w_in.wait()
    pl.semaphore_wait(barrier, len(partners))
    for dz in (8, 4, -4):
        piece(a0, b0, y, at(dz=dz))
    for dy in over_y:
        piece(a0, b0, y, at(dy=dy))

    lax.fori_loop(2, 4, heads, 0)

    for dy in over_y:
        got_piece(a0, b0, turn(y, dy))
    for dz in (1, -1, two):
        unit = wb.at[a0, b0, :, c]
        send(unit, unit, wu.at[b0], at(dz=dz))
    for r in (1, -1, 2):
        a = turn(a0, r)
        got_piece(a, b0, y)
        for dy in over_y:
            piece(a, b0, y, at(dy=dy))
        for dz in (1, -1, two):
            piece(a, b0, y, at(dz=dz))

    near = (1, -1, -two)

    def relay(dz):
        a, b = group(dz)
        for r in (1, -1, 2):
            ar = turn(a, r)
            got_piece(ar, b, y)
            for dy in over_y:
                piece(ar, b, y, at(dy=dy))

    def whole(dz):
        a, b = group(dz)
        if isinstance(dz, int) and dz == 0:
            pass
        else:
            got(wb.at[a, b, :, c], wu.at[b])
        for r in (1, -1, 2):
            for dy in over_y:
                got_piece(turn(a, r), b, turn(y, dy))
        return b

    def across(b, s):
        copy = pltpu.make_async_remote_copy(src_ref=wb.at[:, b, :, c], dst_ref=wb.at[:, b, :, c], send_sem=fs.at[s],
                                            recv_sem=fr.at[s], device_id=at(dc=1), device_id_type=MESH)
        copy.start()
        sent.append(copy)

    def across_in(b, s):
        other = wb.at[:, b, :, 1 - c]
        got(other, fr.at[s])

    def project(b, s):
        for r in (2, 1, 3, 0):
            a = turn(x, r)
            w = wb[a, b].reshape(128, FEAT)
            part = lax.dot_general(att[...], w, TRANS, preferred_element_type=jnp.float32)
            if r == 0:
                own[s] = part
            else:
                xs[s, r - 1] = part.astype(jnp.bfloat16)
                copy = pltpu.make_async_remote_copy(src_ref=xs.at[s, r - 1], dst_ref=xr.at[s, r - 1],
                                                    send_sem=xss.at[s, r - 1], recv_sem=xrs.at[s, r - 1],
                                                    device_id=at(dx=r), device_id_type=MESH)
                copy.start()
                sent.append(copy)

    def finish(b, s):
        total = own[s]
        for r in range(3):
            got(xr.at[s, r], xrs.at[s, r])
            total = total + xr[s, r].astype(jnp.float32)
        o_ref[:, pl.ds(pl.multiple_of(b * 128, 128), 128)] = total.astype(jnp.bfloat16)

    relay(near[0])
    relay(near[1])
    b_0 = whole(0)
    across(b_0, 0)
    relay(near[2])
    across_in(b_0, 0)
    project(b_0, 0)
    bs = [b_0]
    for s in range(1, 4):
        b = whole(near[s - 1])
        across(b, s)
        across_in(b, s)
        project(b, s)
        bs.append(b)
    for s in range(4):
        finish(bs[s], s)
    for copy in sent:
        copy.wait_send()


def shards(queries, keys, values, out_weight, span_start, span_len):
    any_spec = pl.BlockSpec(memory_space=pl.ANY)
    smem = pl.BlockSpec(memory_space=pltpu.SMEM)
    bf16, f32 = jnp.bfloat16, jnp.float32
    dma = pltpu.SemaphoreType.DMA
    return pl.pallas_call(
        kernel,
        out_shape=jax.ShapeDtypeStruct((SEQ, 512), bf16),
        in_specs=[smem, smem, any_spec, any_spec, any_spec, any_spec],
        out_specs=pl.BlockSpec(memory_space=pltpu.VMEM),
        scratch_shapes=[
            pltpu.VMEM((SEQ, FEAT), bf16),
            pltpu.VMEM((SEQ, FEAT), bf16),
            pltpu.VMEM((SEQ, FEAT), bf16),
            pltpu.VMEM((SEQ, FEAT), bf16),
            pltpu.VMEM((SEQ, SEQ), f32),
            pltpu.VMEM((4, 4, 4, 2, 16, FEAT), bf16),
            pltpu.VMEM((4, SEQ, 128), f32),
            pltpu.VMEM((4, 3, SEQ, 128), bf16),
            pltpu.VMEM((4, 3, SEQ, 128), bf16),
            dma((3, 4)), dma, dma((4, 4, 4)), dma((4,)), dma((64,)), dma((4,)), dma((4,)), dma((4, 3)), dma((4, 3)),
        ],
        compiler_params=pltpu.CompilerParams(
            collective_id=0, has_side_effects=True, vmem_limit_bytes=63 << 20
        ),
        name="attend_project",
    )(span_start, span_len, queries, keys, values, out_weight.T)


def solution(mesh):
    placed = (P("dp", "mp"), P("dp", "mp"), P("dp", "mp"), P("mp", "dp"), P("dp"), P("dp"))
    return jax.shard_map(shards, mesh=mesh, in_specs=placed, out_specs=P("dp", "mp"), check_vma=False)
```

time: 164 us -> 67.4 us (0.41)
  waiting for transfers between devices: 88.6 us -> 0 us
  Pallas kernels: 0 us -> 64 us
  blocking collectives: 39.5 us -> 0 us
  between operations: 14.8 us -> 1.3 us
  matrix products: 8.99 us -> 0 us
  other arithmetic: 7.13 us -> 0 us
  local copies, waits for them, and re-layouts: 4.95 us -> 1.87 us
    all_gather x2 -> x0, waiting for transfers between devices: 88.6 us -> none  [stacked_from(): parts = lax.all_gather(parts, axes[k])]
    pallas_call x0 -> x1, Pallas kernels: none -> 64 us  [shards(): pl.pallas_call(kernel, out_shape=jax.ShapeDtypeStruct((SEQ, 512), bf16),...]
    all_to_all x1 -> x0, blocking collectives: 28.7 us -> none  [sent_and_summed(): parts = lax.all_to_all(cut_along(value, dim, size), axis, 0, 0, tiled=True)]
    all_gather x1 -> x0, blocking collectives: 10.8 us -> none  [stacked_from(): parts = lax.all_gather(parts, axes[k])]
    dot_general x3 -> x0, matrix products: 8.99 us -> none  [the longest x1 4.12 us: attend_local(): jnp.einsum('hqk,khd->qhd', weights, value_h, preferred_element_type=jnp.f...]
    sub x1 -> x0, other arithmetic: 5.71 us -> none  [attend_local(): expo = jnp.exp(scores - top)]
    transpose x1 -> x0, local copies, waits for them, and re-layouts: 2.63 us -> none  [stacked_from(): parts = parts.transpose(*back, *range(len(axes), parts.ndim))]
    unnamed x2 -> x1, local copies, waits for them, and re-layouts: 0.01 us -> 1.87 us
  transfers between devices with their start and end apart: 2 -> 0, of which waited for: 2 -> 0; matrix products, arithmetic and copies ran while one was open for 9% -> 0% of each run, Pallas kernels for 0% -> 0%
where the time goes in v1:
time: 67.4 us; the launch traced here: 67.2 us
  Pallas kernels  64 us (95%)
  local copies, waits for them, and re-layouts  1.87 us (3%)
  between operations  1.3 us (2%)
    pallas_call x1, Pallas kernels, shards(): pl.pallas_call(kernel, out_shape=jax.ShapeDtypeStruct((SEQ, 512), bf16),...  64 us
    unnamed x1, local copies, waits for them, and re-layouts  1.87 us

profile of v1, /device:TPU:1, one launch (start us, length us, event | category | flops | bytes accessed | tf_op | source)
XLA Modules:
  0.0 67.2 jit_solution(9817184045526553393)
XLA Ops:
  1.3 64.0 %attend_project.1 = bf16[512,512]{1,0:T(8,128)(2,1)} custom-call(s32[1]{0:T(128)S(6)} %copy.8.start_ref, s32[1]{0:T(128)S(6)} %copy.9.len_ref, bf16[512,1024]{1,0:T(8,128)(2,1)} %q_hbm.1, bf16[512,1024]{1,0:T(8,128)(2,1)} %k_hbm.1, bf16[512,1024]{1,0:T(8,128)(2,1)} %v_hbm.1, bf16[16,1024]{1,0:T(8,128)(2,1)} %bitcast.1), custom_call_target="tpu_custom_call" | custom-call | tf_op jit(solution)/shard_map/attend_project/pallas_call | solution.py:215
  65.3 1.9 %copy.10 = bf16[512,512]{1,0:T(8,128)(2,1)} copy(bf16[512,512]{1,0:T(8,128)(2,1)} %attend_project.1) | data formatting | bytes 1048576

commit v2 on v1

v2 whole, which is shorter than its diff:
```python
import functools

import jax
import jax.numpy as jnp
from jax import lax
from jax.experimental import pallas as pl
from jax.experimental.pallas import tpu as pltpu
from jax.sharding import PartitionSpec as P

MESH = pl.DeviceIdType.MESH
HD = 128
BLK = 128
SEQ = 512
HEADS = 8
FEAT = HEADS * HD
NEG = -1e30
SCALE = 1.4426950408889634 / (128.0**0.5)
TRANS = (((1,), (1,)), ((), ()))
BEFORE, CUT = 2, 7


def attend_head(q_ref, k_ref, v_ref, att, bias, h):
    cols = pl.ds(pl.multiple_of(h * HD, HD), HD)
    key = k_ref[:, cols]
    val = v_ref[:, cols]
    for qb in range(SEQ // BLK):
        rows = pl.ds(qb * BLK, BLK)
        keys = BLK if qb == 0 else SEQ
        s = lax.dot_general(q_ref[rows, cols], key[:keys], TRANS, preferred_element_type=jnp.float32)
        s = s + bias[rows, pl.ds(0, keys)]
        top = jnp.max(s, axis=-1, keepdims=True)
        p = jnp.exp2((s - top) * SCALE)
        total = jnp.sum(p, axis=-1, keepdims=True)
        o = jnp.dot(p.astype(jnp.bfloat16), val[:keys], preferred_element_type=jnp.float32)
        att[rows, cols] = (o / total).astype(jnp.bfloat16)


def kernel(start_ref, len_ref, q_hbm, k_hbm, v_hbm, w_hbm, o_ref,
           q, k, v, att, bias, wb, own, keep, xs, xm, xf, xr,
           qsem, wsem, wr, wl, wh, wu, wuh, ws, fs, fr, xss, xrs, xms):
    dp, x = lax.axis_index("dp"), lax.axis_index("mp")
    c = lax.rem(dp, 2)
    y = lax.rem(lax.div(dp, 2), 4)
    z = lax.div(dp, 8)
    two = 2 - 4 * lax.rem(z, 2)

    def at(dz=0, dy=0, dx=0, dc=0):
        zz, yy = lax.rem(z + dz + 16, 16), lax.rem(y + dy + 4, 4)
        return ((zz * 4 + yy) * 2 + lax.rem(c + dc, 2), lax.rem(x + dx + 4, 4))

    def turn(a, r):
        return lax.rem(a + r + 4, 4)

    shift = (0, 1, -1, -two)
    zs = [lax.rem(z + d + 16, 16) for d in shift]
    a_of = [lax.div(zz, 4) for zz in zs]
    b_of = [lax.rem(zz, 4) for zz in zs]
    over_y = (1, -1, 2)
    near_z = (1, -1, two)
    lo, hi = pl.ds(0, FEAT // 2), pl.ds(FEAT // 2, FEAT // 2)

    barrier = pltpu.get_barrier_semaphore()
    partners = [at(dz=4), at(dz=-4), at(dz=1), at(dz=-1), at(dz=2), at(dz=-2),
                at(dy=1), at(dy=-1), at(dy=2), at(dx=1), at(dx=2), at(dx=3), at(dc=1)]
    for who in partners:
        pl.semaphore_signal(barrier, inc=1, device_id=who, device_id_type=MESH)

    w_in = pltpu.make_async_copy(w_hbm, wb.at[a_of[0], b_of[0], y, c], wsem)
    w_in.start()

    def inputs(i):
        cols = pl.ds(pl.multiple_of(i * 256, 256), 256)
        return [pltpu.make_async_copy(src.at[:, cols], dst.at[:, cols], qsem.at[n, i])
                for n, (src, dst) in enumerate(((q_hbm, q), (k_hbm, k), (v_hbm, v)))]

    for i in range(4):
        for copy in inputs(i):
            copy.start()

    row = lax.broadcasted_iota(jnp.int32, (SEQ, SEQ), 0)
    col = lax.broadcasted_iota(jnp.int32, (SEQ, SEQ), 1)
    first = start_ref[0] * BLK
    last = jnp.minimum(start_ref[0] + len_ref[0], SEQ // BLK) * BLK
    image_row = (row >= first) & (row < last)
    image_col = (col >= first) & (col < last)
    bias[...] = jnp.where(image_row, jnp.where(image_col, 0.0, NEG), jnp.where(col <= row, 0.0, NEG))

    def heads(from_head, to_head):
        def body(h, carry):
            @pl.when(lax.rem(h, 2) == 0)
            def _():
                for copy in inputs(lax.div(h, 2)):
                    copy.wait()

            attend_head(q, k, v, att, bias, h)
            return carry

        lax.fori_loop(from_head, to_head, body, 0)

    sent = []

    def send(ref, sem, who):
        copy = pltpu.make_async_remote_copy(src_ref=ref, dst_ref=ref, send_sem=ws.at[len(sent)], recv_sem=sem,
                                            device_id=who, device_id_type=MESH)
        copy.start()
        sent.append(copy)

    def got(ref, sem):
        pltpu.make_async_remote_copy(src_ref=ref, dst_ref=ref, send_sem=ws.at[0], recv_sem=sem,
                                     device_id=at(dc=1), device_id_type=MESH).wait_recv()

    def slot(n, r, dy):
        return turn(a_of[n], r), b_of[n], turn(y, dy)

    def whole(n, r, dy):
        i = slot(n, r, dy)
        return wb.at[i[0], i[1], i[2], c], wr.at[i[0], i[1], i[2]]

    def low(n, r, dy):
        i = slot(n, r, dy)
        return wb.at[i[0], i[1], i[2], c, :, lo], wl.at[i[0], i[1], i[2]]

    def high(n, r, dy):
        i = slot(n, r, dy)
        return wb.at[i[0], i[1], i[2], c, :, hi], wh.at[i[0], i[1], i[2]]

    def unit(n, r):
        i = slot(n, r, 0)
        return wb.at[i[0], i[1], :, c], wu.at[i[1]]

    def unit_high(n, r):
        i = slot(n, r, 0)
        return wb.at[i[0], i[1], :, c, :, hi], wuh.at[i[1]]

    def to_y(what):
        for dy in over_y:
            send(*what, at(dy=dy))

    def to_z(what):
        for dz in near_z:
            send(*what, at(dz=dz))

    blocks = []

    def across(n, r):
        i = slot(n, r, 0)
        ref = wb.at[i[0], i[1], :, c]
        m = len(blocks)
        copy = pltpu.make_async_remote_copy(src_ref=ref, dst_ref=ref, send_sem=fs.at[m], recv_sem=fr.at[m],
                                            device_id=at(dc=1), device_id_type=MESH)
        copy.start()
        blocks.append((n, r, copy))

    half = SEQ // 2
    top, low_half = pl.ds(0, half), pl.ds(half, half)

    def hop(m, dst, rows, k, sem, to):
        return pltpu.make_async_remote_copy(src_ref=xs.at[m, rows], dst_ref=dst, send_sem=xss.at[m, k], recv_sem=sem,
                                            device_id=(dp, to), device_id_type=MESH)

    def to_dest(n, m, side, k):
        a = turn(a_of[n], blocks[m][1])
        rows = top if k == 0 else low_half
        return hop(m, xr.at[n, side, k], rows, k, xrs.at[n, side, k], a)

    def to_dest_f(n, m, side, k):
        a = turn(a_of[n], blocks[m][1])
        return pltpu.make_async_remote_copy(src_ref=xf.at[m], dst_ref=xr.at[n, side, k], send_sem=xss.at[m, k],
                                            recv_sem=xrs.at[n, side, k], device_id=(dp, a), device_id_type=MESH)

    def to_middle(m, k):
        rows = top if k == 0 else low_half
        return hop(m, xm.at[m], rows, k, xms.at[m], turn(x, -1 if k == 0 else 1))

    def project(*ms):
        ws_in = []
        for m in ms:
            n, r, _ = blocks[m]
            a, b, _ = slot(n, r, 0)
            got(wb.at[a, b, :, 1 - c], fr.at[m])
            ws_in.append(wb[a, b].reshape(128, FEAT))
        w = ws_in[0] if len(ws_in) == 1 else jnp.concatenate(ws_in, axis=0)
        parts = lax.dot_general(att[...], w, TRANS, preferred_element_type=jnp.float32)
        for k, m in enumerate(ms):
            n, r, _ = blocks[m]
            a = turn(a_of[n], r)
            part = parts[:, k * 128:(k + 1) * 128]

            away = turn(a, -x)

            @pl.when(away == 0)
            def _(n=n, part=part):
                own[n] = part

            @pl.when(away != 0)
            def _(m=m, part=part):
                xs[m] = part.astype(jnp.bfloat16)

            @pl.when(away == 1)
            def _(n=n, m=m, part=part):
                keep[m] = part[half:]
                to_dest(n, m, 1, 0).start()

            @pl.when(away == 3)
            def _(n=n, m=m, part=part):
                keep[m] = part[:half]
                to_dest(n, m, 0, 1).start()

            @pl.when(away == 2)
            def _(m=m):
                to_middle(m, 0).start()
                to_middle(m, 1).start()

    def forward(*ms):
        for m in ms:
            n, r, _ = blocks[m]
            away = turn(turn(a_of[n], r), -x)
            for here, side, k in ((1, 1, 1), (3, 0, 0)):
                @pl.when(away == here)
                def _(n=n, m=m, side=side, k=k):
                    got(xm.at[m], xms.at[m])
                    rows = top if k == 0 else low_half
                    fs_m = (keep[m] + xm[m].astype(jnp.float32)).astype(jnp.bfloat16)
                    xf[m] = fs_m
                    to_dest_f(n, m, side, k).start()

    heads(0, BEFORE)
    w_in.wait()
    pl.semaphore_wait(barrier, len(partners))
    for dz in (4, -4):
        send(*whole(0, 0, 0), at(dz=dz))
    to_y(whole(0, 0, 0))
    to_z(whole(0, 0, 0))
    heads(BEFORE, CUT)
    got(*whole(0, 1, 0))
    got(*whole(0, -1, 0))
    i = slot(0, -1, 0)
    send(wb.at[i[0], i[1], i[2], c, :, lo], wl.at[i[0], i[1], i[2]], at(dz=4))
    i = slot(0, 1, 0)
    send(wb.at[i[0], i[1], i[2], c, :, hi], wh.at[i[0], i[1], i[2]], at(dz=-4))
    to_y(whole(0, 1, 0))
    to_z(whole(0, -1, 0))
    to_y(whole(0, -1, 0))
    for n in (1, 2, 3):
        got(*whole(n, 0, 0))
        to_y(whole(n, 0, 0))
    for dy in over_y:
        got(*whole(0, 0, dy))
    across(0, 0)
    heads(CUT, HEADS)
    project(0)
    for dy in over_y:
        got(*whole(0, 1, dy))
    to_z(unit(0, 1))
    across(0, 1)
    got(*low(0, 2, 0))
    to_z(low(0, 2, 0))
    to_y(low(0, 2, 0))
    got(*high(0, 2, 0))
    to_y(high(0, 2, 0))
    for dy in over_y:
        got(*whole(0, -1, dy))
    across(0, -1)
    for n in (1, 2, 3):
        got(*whole(n, -1, 0))
        to_y(whole(n, -1, 0))
    project(1, 2)
    for n in (1, 2, 3):
        for dy in over_y:
            got(*whole(n, 0, dy))
        across(n, 0)
    forward(0)
    for dy in over_y:
        got(*high(0, 2, dy))
    to_z(unit_high(0, 2))
    for n in (1, 2, 3):
        got(*low(n, 2, 0))
        to_y(low(n, 2, 0))
    for dy in over_y:
        got(*low(0, 2, dy))
    across(0, 2)
    project(3, 4, 5, 6)
    forward(1, 2)
    for n in (1, 2, 3):
        got(*unit(n, 1))
        across(n, 1)
    for n in (1, 2, 3):
        for dy in over_y:
            got(*whole(n, -1, dy))
        across(n, -1)
    project(7, 8, 9, 10)
    forward(3, 4)
    project(11, 12)
    forward(5, 6)
    for n in (1, 2, 3):
        got(*unit_high(n, 2))
        for dy in over_y:
            got(*low(n, 2, dy))
        across(n, 2)
    forward(7, 8)
    project(13, 14, 15)
    forward(9, 10, 11, 12, 13, 14, 15)
    for n in range(4):
        cols = pl.ds(pl.multiple_of(b_of[n] * 128, 128), 128)
        for k, rows in ((0, top), (1, low_half)):
            total = own[n, rows]
            for side in range(2):
                got(xr.at[n, side, k], xrs.at[n, side, k])
                total = total + xr[n, side, k].astype(jnp.float32)
            o_ref[rows, cols] = total.astype(jnp.bfloat16)
    for copy in sent:
        copy.wait_send()
    for m, (n, r, copy) in enumerate(blocks):
        copy.wait_send()
        away = turn(turn(a_of[n], r), -x)

        @pl.when(away == 1)
        def _(n=n, m=m):
            to_dest(n, m, 1, 0).wait_send()
            to_dest_f(n, m, 1, 1).wait_send()

        @pl.when(away == 3)
        def _(n=n, m=m):
            to_dest(n, m, 0, 1).wait_send()
            to_dest_f(n, m, 0, 0).wait_send()

        @pl.when(away == 2)
        def _(m=m):
            to_middle(m, 0).wait_send()
            to_middle(m, 1).wait_send()


def shards(queries, keys, values, out_weight, span_start, span_len):
    any_spec = pl.BlockSpec(memory_space=pl.ANY)
    smem = pl.BlockSpec(memory_space=pltpu.SMEM)
    bf16, f32 = jnp.bfloat16, jnp.float32
    dma = pltpu.SemaphoreType.DMA
    return pl.pallas_call(
        kernel,
        out_shape=jax.ShapeDtypeStruct((SEQ, 512), bf16),
        in_specs=[smem, smem, any_spec, any_spec, any_spec, any_spec],
        out_specs=pl.BlockSpec(memory_space=pltpu.VMEM),
        scratch_shapes=[
            pltpu.VMEM((SEQ, FEAT), bf16),
            pltpu.VMEM((SEQ, FEAT), bf16),
            pltpu.VMEM((SEQ, FEAT), bf16),
            pltpu.VMEM((SEQ, FEAT), bf16),
            pltpu.VMEM((SEQ, SEQ), f32),
            pltpu.VMEM((4, 4, 4, 2, 16, FEAT), bf16),
            pltpu.VMEM((4, SEQ, 128), f32),
            pltpu.VMEM((16, SEQ // 2, 128), f32),
            pltpu.VMEM((16, SEQ, 128), bf16),
            pltpu.VMEM((16, SEQ // 2, 128), bf16),
            pltpu.VMEM((16, SEQ // 2, 128), bf16),
            pltpu.VMEM((4, 2, 2, SEQ // 2, 128), bf16),
            dma((3, 4)), dma, dma((4, 4, 4)), dma((4, 4, 4)), dma((4, 4, 4)), dma((4,)), dma((4,)), dma((64,)),
            dma((16,)), dma((16,)), dma((16, 2)), dma((4, 2, 2)), dma((16,)),
        ],
        compiler_params=pltpu.CompilerParams(
            collective_id=0, has_side_effects=True, vmem_limit_bytes=63 << 20
        ),
        name="attend_project",
    )(span_start, span_len, queries, keys, values, out_weight.T)


def solution(mesh):
    placed = (P("dp", "mp"), P("dp", "mp"), P("dp", "mp"), P("mp", "dp"), P("dp"), P("dp"))
    return jax.shard_map(shards, mesh=mesh, in_specs=placed, out_specs=P("dp", "mp"), check_vma=False)
```

time: 67.4 us -> 62.2 us (0.923); the launches traced: 67.2 us -> 61.2 us
  Pallas kernels: 64 us -> 58 us
    pallas_call x1, Pallas kernels: 64 us -> 58 us  [shards(): pl.pallas_call(kernel, out_shape=jax.ShapeDtypeStruct((SEQ, 512), bf16),...]
where the time goes in v2:
time: 62.2 us; the launch traced here: 61.2 us
  Pallas kernels  58 us (93%)
  local copies, waits for them, and re-layouts  1.87 us (3%)
  between operations  1.3 us (2%)
    pallas_call x1, Pallas kernels, shards(): pl.pallas_call(kernel, out_shape=jax.ShapeDtypeStruct((SEQ, 512), bf16),...  58 us
    unnamed x1, local copies, waits for them, and re-layouts  1.87 us

profile of v2, /device:TPU:1, one launch (start us, length us, event | category | flops | bytes accessed | tf_op | source)
XLA Modules:
  0.0 61.2 jit_solution(5315501283849870170)
XLA Ops:
  1.3 58.0 %attend_project.1 = bf16[512,512]{1,0:T(8,128)(2,1)} custom-call(s32[1]{0:T(128)S(6)} %copy.8.start_ref, s32[1]{0:T(128)S(6)} %copy.9.len_ref, bf16[512,1024]{1,0:T(8,128)(2,1)} %q_hbm.1, bf16[512,1024]{1,0:T(8,128)(2,1)} %k_hbm.1, bf16[512,1024]{1,0:T(8,128)(2,1)} %v_hbm.1, bf16[16,1024]{1,0:T(8,128)(2,1)} %bitcast.1), custom_call_target="tpu_custom_call" | custom-call | tf_op jit(solution)/shard_map/attend_project/pallas_call | solution.py:338
  59.3 1.9 %copy.10 = bf16[512,512]{1,0:T(8,128)(2,1)} copy(bf16[512,512]{1,0:T(8,128)(2,1)} %attend_project.1) | data formatting | bytes 1048576

commit v3 on v2

v3 whole, which is shorter than its diff:
```python
import functools

import jax
import jax.numpy as jnp
from jax import lax
from jax.experimental import pallas as pl
from jax.experimental.pallas import tpu as pltpu
from jax.sharding import PartitionSpec as P

MESH = pl.DeviceIdType.MESH
HD = 128
BLK = 128
SEQ = 512
HEADS = 8
FEAT = HEADS * HD
NEG = -1e30
SCALE = 1.4426950408889634 / (128.0**0.5)
TRANS = (((1,), (1,)), ((), ()))
BEFORE, CUT1, CUT2 = 2, 5, 7
VMEM_BYTES = 63 << 20


def attend_head(q_ref, k_ref, v_ref, att, bias, h):
    cols = pl.ds(pl.multiple_of(h * HD, HD), HD)
    key = k_ref[:, cols]
    val = v_ref[:, cols]
    for qb in range(SEQ // BLK):
        rows = pl.ds(qb * BLK, BLK)
        keys = BLK if qb == 0 else SEQ
        s = lax.dot_general(q_ref[rows, cols], key[:keys], TRANS, preferred_element_type=jnp.float32)
        s = s + bias[rows, pl.ds(0, keys)]
        top = jnp.max(s, axis=-1, keepdims=True)
        p = jnp.exp2((s - top) * SCALE)
        total = jnp.sum(p, axis=-1, keepdims=True)
        o = jnp.dot(p.astype(jnp.bfloat16), val[:keys], preferred_element_type=jnp.float32)
        att[rows, cols] = (o / total).astype(jnp.bfloat16)


def kernel(start_ref, len_ref, q_hbm, k_hbm, v_hbm, w_hbm, o_hbm,
           qkv, att, bias, wb, own, keep, xs, xm, xf, xr, out,
           osem, qsem, wsem, here_sem, y_sem, unit_sem, ws, fs, fr, xss, xrs, xms):
    dp, x = lax.axis_index("dp"), lax.axis_index("mp")
    c = lax.rem(dp, 2)
    y = lax.rem(lax.div(dp, 2), 4)
    z = lax.div(dp, 8)
    two = 2 - 4 * lax.rem(z, 2)

    def at(dz=0, dy=0, dx=0, dc=0):
        zz, yy = lax.rem(z + dz + 16, 16), lax.rem(y + dy + 4, 4)
        return ((zz * 4 + yy) * 2 + lax.rem(c + dc, 2), lax.rem(x + dx + 4, 4))

    def turn(a, r):
        return lax.rem(a + r + 4, 4)

    shift = (0, 1, -1, -two)
    zs = [lax.rem(z + d + 16, 16) for d in shift]
    a_of = [lax.div(zz, 4) for zz in zs]
    b_of = [lax.rem(zz, 4) for zz in zs]
    over_y = (1, -1, 2)
    near_z = (1, -1, two)
    lo, hi = pl.ds(0, FEAT // 2), pl.ds(FEAT // 2, FEAT // 2)

    barrier = pltpu.get_barrier_semaphore()
    partners = [at(dz=4), at(dz=-4), at(dz=1), at(dz=-1), at(dz=2), at(dz=-2),
                at(dy=1), at(dy=-1), at(dy=2), at(dx=1), at(dx=2), at(dx=3), at(dc=1)]
    for who in partners:
        pl.semaphore_signal(barrier, inc=1, device_id=who, device_id_type=MESH)

    w_in = pltpu.make_async_copy(w_hbm, wb.at[a_of[0], b_of[0], y, c], wsem)
    w_in.start()

    def quarter(i):
        return pl.ds(pl.multiple_of(i * 256, 256), 256)

    for i in range(4):
        for n, src in enumerate((q_hbm, k_hbm, v_hbm)):
            pltpu.make_async_copy(src.at[:, quarter(i)], qkv.at[n, :, quarter(i)], qsem.at[i]).start()

    row = lax.broadcasted_iota(jnp.int32, (SEQ, SEQ), 0)
    col = lax.broadcasted_iota(jnp.int32, (SEQ, SEQ), 1)
    first = start_ref[0] * BLK
    last = jnp.minimum(start_ref[0] + len_ref[0], SEQ // BLK) * BLK
    image_row = (row >= first) & (row < last)
    image_col = (col >= first) & (col < last)
    bias[...] = jnp.where(image_row, jnp.where(image_col, 0.0, NEG), jnp.where(col <= row, 0.0, NEG))

    def heads(from_head, to_head):
        def body(h, carry):
            @pl.when(lax.rem(h, 2) == 0)
            def _():
                i = lax.div(h, 2)
                pltpu.make_async_copy(qkv.at[:, :, quarter(i)], qkv.at[:, :, quarter(i)], qsem.at[i]).wait()

            attend_head(qkv.at[0], qkv.at[1], qkv.at[2], att, bias, h)
            return carry

        lax.fori_loop(from_head, to_head, body, 0)

    groups = []

    def send(ref, sem, whom, all_of):
        n = len(groups)
        for who in whom:
            pltpu.make_async_remote_copy(src_ref=ref, dst_ref=ref, send_sem=ws.at[n], recv_sem=sem,
                                         device_id=who, device_id_type=MESH).start()
        groups.append(all_of)

    def gone(n):
        pltpu.make_async_remote_copy(src_ref=groups[n], dst_ref=groups[n], send_sem=ws.at[n], recv_sem=ws.at[n],
                                     device_id=at(dc=1), device_id_type=MESH).wait_send()

    def got(ref, sem):
        pltpu.make_async_remote_copy(src_ref=ref, dst_ref=ref, send_sem=ws.at[0], recv_sem=sem,
                                     device_id=at(dc=1), device_id_type=MESH).wait_recv()

    every = pl.ds(0, FEAT)
    three = pl.ds(0, 3)
    kind = {(0, 0): (0, every), (1, 0): (1, every), (-1, 0): (2, every), (2, 0): (3, lo), (2, 1): (4, hi)}

    def piece(n, r, part=0):
        a, b = turn(a_of[n], r), b_of[n]
        sem, feats = kind[r, part]
        return wb.at[a, b, y, c, :, feats], sem, wb.at[a, b, three, c, :, feats]

    def to_y(n, r, part=0):
        ref, sem, size = piece(n, r, part)
        send(ref, y_sem.at[b_of[n], sem], [at(dy=dy) for dy in over_y], size)

    def to_z(n, r, part=0):
        ref, sem, size = piece(n, r, part)
        send(ref, here_sem.at[b_of[n], sem], [at(dz=dz) for dz in near_z], size)

    def got_here(n, r, part=0):
        ref, sem, _ = piece(n, r, part)
        got(ref, here_sem.at[b_of[n], sem])

    def got_y(n, r, part=0):
        _, sem, size = piece(n, r, part)
        got(size, y_sem.at[b_of[n], sem])

    def unit(n, r):
        a, b = turn(a_of[n], r), b_of[n]
        sem, feats = (0, every) if r == 1 else (1, hi)
        return wb.at[a, b, :, c, :, feats], unit_sem.at[b, sem], wb.at[three, b, :, c, :, feats]

    def unit_to_z(r):
        ref, sem, size = unit(0, r)
        send(ref, sem, [at(dz=dz) for dz in near_z], size)

    def got_unit(n, r):
        ref, sem, _ = unit(n, r)
        got(ref, sem)

    blocks = []

    def across(n, r, g):
        ref = wb.at[turn(a_of[n], r), b_of[n], :, c]
        pltpu.make_async_remote_copy(src_ref=ref, dst_ref=ref, send_sem=fs, recv_sem=fr.at[g],
                                     device_id=at(dc=1), device_id_type=MESH).start()
        blocks.append((n, r))

    half = SEQ // 2
    top, low_half = pl.ds(0, half), pl.ds(half, half)

    def hop(m, dst, rows, k, sem, to):
        return pltpu.make_async_remote_copy(src_ref=xs.at[m, rows], dst_ref=dst, send_sem=xss, recv_sem=sem,
                                            device_id=(dp, to), device_id_type=MESH)

    def to_dest(n, m, side, k):
        a = turn(a_of[n], blocks[m][1])
        rows = top if k == 0 else low_half
        return hop(m, xr.at[n, side, k], rows, k, xrs.at[n], a)

    def to_dest_f(n, m, side, k):
        a = turn(a_of[n], blocks[m][1])
        return pltpu.make_async_remote_copy(src_ref=xf.at[m], dst_ref=xr.at[n, side, k], send_sem=xss,
                                            recv_sem=xrs.at[n], device_id=(dp, a), device_id_type=MESH)

    def to_middle(m, k):
        rows = top if k == 0 else low_half
        return hop(m, xm.at[m], rows, k, xms.at[m], turn(x, -1 if k == 0 else 1))

    def project(g, *ms):
        got(wb.at[pl.ds(0, len(ms)), 0, :, 1 - c], fr.at[g])
        ws_in = []
        for m in ms:
            n, r = blocks[m]
            ws_in.append(wb[turn(a_of[n], r), b_of[n]].reshape(128, FEAT))
        w = ws_in[0] if len(ws_in) == 1 else jnp.concatenate(ws_in, axis=0)
        parts = lax.dot_general(att[...], w, TRANS, preferred_element_type=jnp.float32)
        for k, m in enumerate(ms):
            n, r = blocks[m]
            a = turn(a_of[n], r)
            part = parts[:, k * 128:(k + 1) * 128]

            away = turn(a, -x)

            @pl.when(away == 0)
            def _(n=n, part=part):
                own[n] = part

            @pl.when(away != 0)
            def _(m=m, part=part):
                xs[m] = part.astype(jnp.bfloat16)

            @pl.when(away == 1)
            def _(n=n, m=m, part=part):
                keep[m] = part[half:]
                to_dest(n, m, 1, 0).start()

            @pl.when(away == 3)
            def _(n=n, m=m, part=part):
                keep[m] = part[:half]
                to_dest(n, m, 0, 1).start()

            @pl.when(away == 2)
            def _(m=m):
                to_middle(m, 0).start()
                to_middle(m, 1).start()

    def forward(*ms):
        for m in ms:
            n, r = blocks[m]
            away = turn(turn(a_of[n], r), -x)
            for here, side, k in ((1, 1, 1), (3, 0, 0)):
                @pl.when(away == here)
                def _(n=n, m=m, side=side, k=k):
                    got(xm.at[m], xms.at[m])
                    rows = top if k == 0 else low_half
                    fs_m = (keep[m] + xm[m].astype(jnp.float32)).astype(jnp.bfloat16)
                    xf[m] = fs_m
                    to_dest_f(n, m, side, k).start()

    heads(0, BEFORE)
    w_in.wait()
    pl.semaphore_wait(barrier, len(partners))
    to_z(0, 0)
    mine = wb.at[a_of[0], b_of[0], y, c]
    n_out = len(groups)
    for dz, sem in ((4, 2), (-4, 1)):
        pltpu.make_async_remote_copy(src_ref=mine, dst_ref=mine, send_sem=ws.at[n_out],
                                     recv_sem=here_sem.at[b_of[0], sem],
                                     device_id=at(dz=dz), device_id_type=MESH).start()
    groups.append(wb.at[a_of[0], b_of[0], pl.ds(0, 2), c])
    to_y(0, 0)
    heads(BEFORE, CUT1)
    for n in (1, 2, 3):
        got_here(n, 0)
        to_y(n, 0)
    heads(CUT1, CUT2)
    got_here(0, 1)
    got_here(0, -1)
    n_out = len(groups)
    for r, dz, feats, sem in ((-1, 4, lo, 3), (1, -4, hi, 4)):
        ref = wb.at[turn(a_of[0], r), b_of[0], y, c, :, feats]
        pltpu.make_async_remote_copy(src_ref=ref, dst_ref=ref, send_sem=ws.at[n_out],
                                     recv_sem=here_sem.at[b_of[0], sem],
                                     device_id=at(dz=dz), device_id_type=MESH).start()
    groups.append(wb.at[a_of[0], b_of[0], y, c])
    to_y(0, 1)
    to_z(0, -1)
    to_y(0, -1)
    got_y(0, 0)
    across(0, 0, 0)
    heads(CUT2, HEADS)
    project(0, 0)
    for n in (1, 2, 3):
        got_y(n, 0)
        across(n, 0, 1)
    got_y(0, 1)
    unit_to_z(1)
    across(0, 1, 1)
    got_here(0, 2)
    to_z(0, 2)
    to_y(0, 2)
    got_here(0, 2, 1)
    to_y(0, 2, 1)
    for n in (1, 2, 3):
        got_here(n, -1)
        to_y(n, -1)
    project(1, 1, 2, 3, 4)
    got_y(0, -1)
    across(0, -1, 2)
    forward(0)
    for n in (1, 2, 3):
        got_here(n, 2)
        to_y(n, 2)
    got_y(0, 2, 1)
    unit_to_z(2)
    project(2, 5)
    got_y(0, 2)
    across(0, 2, 3)
    for n in (1, 2, 3):
        got_unit(n, 1)
        across(n, 1, 3)
    forward(1, 2)
    for n in (1, 2, 3):
        got_y(n, -1)
        across(n, -1, 4)
    project(3, 6, 7, 8, 9)
    forward(3, 4, 5)
    for n in (1, 2, 3):
        got_unit(n, 2)
        got_y(n, 2)
        across(n, 2, 5)
    project(4, 10, 11, 12)
    project(5, 13, 14, 15)
    for m in range(6, 16):
        forward(m)
        if m > 8:
            for n in range(3 * m - 27, 3 * m - 24):
                gone(n)
    for n in range(21, len(groups)):
        gone(n)
    for n in range(4):
        cols = pl.ds(pl.multiple_of(b_of[n] * 128, 128), 128)
        got(xr.at[n], xrs.at[n])
        for k, rows in ((0, top), (1, low_half)):
            total = own[n, rows]
            for side in range(2):
                total = total + xr[n, side, k].astype(jnp.float32)
            out[rows, cols] = total.astype(jnp.bfloat16)
        pltpu.make_async_copy(out.at[:, cols], o_hbm.at[:, cols], osem).start()
    both = wb.at[:, :, :, c]
    pltpu.make_async_remote_copy(src_ref=both, dst_ref=both, send_sem=fs, recv_sem=fs,
                                 device_id=at(dc=1), device_id_type=MESH).wait_send()
    most = xs.at[pl.ds(0, 12)]
    pltpu.make_async_remote_copy(src_ref=most, dst_ref=most, send_sem=xss, recv_sem=xss,
                                 device_id=at(dc=1), device_id_type=MESH).wait_send()
    pltpu.make_async_copy(out, o_hbm, osem).wait()


def shards(queries, keys, values, out_weight, span_start, span_len):
    hbm = pl.BlockSpec(memory_space=pltpu.HBM)
    smem = pl.BlockSpec(memory_space=pltpu.SMEM)
    bf16, f32 = jnp.bfloat16, jnp.float32
    dma = pltpu.SemaphoreType.DMA
    return pl.pallas_call(
        kernel,
        out_shape=jax.ShapeDtypeStruct((SEQ, 512), bf16),
        in_specs=[smem, smem, hbm, hbm, hbm, hbm],
        out_specs=hbm,
        scratch_shapes=[
            pltpu.VMEM((3, SEQ, FEAT), bf16),
            pltpu.VMEM((SEQ, FEAT), bf16),
            pltpu.VMEM((SEQ, SEQ), f32),
            pltpu.VMEM((4, 4, 4, 2, 16, FEAT), bf16),
            pltpu.VMEM((4, SEQ, 128), f32),
            pltpu.VMEM((16, SEQ // 2, 128), f32),
            pltpu.VMEM((16, SEQ, 128), bf16),
            pltpu.VMEM((16, SEQ // 2, 128), bf16),
            pltpu.VMEM((16, SEQ // 2, 128), bf16),
            pltpu.VMEM((4, 2, 2, SEQ // 2, 128), bf16),
            pltpu.VMEM((SEQ, 512), bf16),
            dma, dma((4,)), dma, dma((4, 5)), dma((4, 5)), dma((4, 2)), dma((24,)), dma, dma((6,)), dma, dma((4,)), dma((16,)),
        ],
        compiler_params=pltpu.CompilerParams(
            collective_id=0, has_side_effects=True, vmem_limit_bytes=VMEM_BYTES
        ),
        name="attend_project",
    )(span_start, span_len, queries, keys, values, out_weight.T)


def solution(mesh):
    placed = (P("dp", "mp"), P("dp", "mp"), P("dp", "mp"), P("mp", "dp"), P("dp"), P("dp"))
    return jax.shard_map(shards, mesh=mesh, in_specs=placed, out_specs=P("dp", "mp"), check_vma=False)
```

time: 62.2 us -> 58.2 us (0.936)
  the two profiles are of different devices: /device:TPU:1 before, /device:TPU:4 now
where the time goes in v3:
time: 58.2 us; the launch traced here: 58.1 us
  Pallas kernels  54.9 us (94%)
  local copies, waits for them, and re-layouts  1.87 us (3%)
  between operations  1.3 us (2%)
    pallas_call x1, Pallas kernels, shards(): pl.pallas_call(kernel, out_shape=jax.ShapeDtypeStruct((SEQ, 512), bf16),...  54.9 us
    unnamed x1, local copies, waits for them, and re-layouts  1.87 us

profile of v3, /device:TPU:4, one launch (start us, length us, event | category | flops | bytes accessed | tf_op | source)
XLA Modules:
  0.0 58.1 jit_solution(12858113714778873265)
XLA Ops:
  1.3 54.9 %attend_project.1 = bf16[512,512]{1,0:T(8,128)(2,1)} custom-call(s32[1]{0:T(128)S(6)} %copy.8.start_ref, s32[1]{0:T(128)S(6)} %copy.9.len_ref, bf16[512,1024]{1,0:T(8,128)(2,1)} %q_hbm.1, bf16[512,1024]{1,0:T(8,128)(2,1)} %k_hbm.1, bf16[512,1024]{1,0:T(8,128)(2,1)} %v_hbm.1, bf16[16,1024]{1,0:T(8,128)(2,1)} %bitcast.1), custom_call_target="tpu_custom_call" | custom-call | tf_op jit(solution)/shard_map/attend_project/pallas_call | solution.py:338
  56.2 1.9 %copy.10 = bf16[512,512]{1,0:T(8,128)(2,1)} copy(bf16[512,512]{1,0:T(8,128)(2,1)} %attend_project.1) | data formatting | bytes 1048576

commit v4 on v3

--- a/solution.py
+++ b/solution.py
@@ -17,7 +17,7 @@
 SCALE = 1.4426950408889634 / (128.0**0.5)
 TRANS = (((1,), (1,)), ((), ()))
 BEFORE, CUT1, CUT2 = 2, 5, 7
-VMEM_BYTES = 63 << 20
+VMEM_BYTES = 53 << 20
 
 
 def attend_head(q_ref, k_ref, v_ref, att, bias, h):
@@ -138,18 +138,24 @@
         _, sem, size = piece(n, r, part)
         got(size, y_sem.at[b_of[n], sem])
 
-    def unit(n, r):
+    def rest(n, r):
+        sem, feats = (0, every) if r == 1 else (1, hi)
         a, b = turn(a_of[n], r), b_of[n]
-        sem, feats = (0, every) if r == 1 else (1, hi)
-        return wb.at[a, b, :, c, :, feats], unit_sem.at[b, sem], wb.at[three, b, :, c, :, feats]
-
-    def unit_to_z(r):
-        ref, sem, size = unit(0, r)
-        send(ref, sem, [at(dz=dz) for dz in near_z], size)
-
-    def got_unit(n, r):
-        ref, sem, _ = unit(n, r)
-        got(ref, sem)
+        return a, b, feats, unit_sem.at[b, sem]
+
+    def rest_to_z(r):
+        a, b, feats, sem = rest(0, r)
+        m = len(groups)
+        for dy in over_y:
+            ref = wb.at[a, b, turn(y, dy), c, :, feats]
+            for dz in near_z:
+                pltpu.make_async_remote_copy(src_ref=ref, dst_ref=ref, send_sem=ws.at[m], recv_sem=sem,
+                                             device_id=at(dz=dz), device_id_type=MESH).start()
+        groups.append(wb.at[three, b, three, c, :, feats])
+
+    def got_rest(n, r):
+        a, b, feats, sem = rest(n, r)
+        got(wb.at[a, b, three, c, :, feats], sem)
 
     blocks = []
 
@@ -258,52 +264,56 @@
                                      device_id=at(dz=dz), device_id_type=MESH).start()
     groups.append(wb.at[a_of[0], b_of[0], y, c])
     to_y(0, 1)
+    to_z(0, 1)
+    to_y(0, -1)
     to_z(0, -1)
-    to_y(0, -1)
     got_y(0, 0)
     across(0, 0, 0)
     heads(CUT2, HEADS)
-    project(0, 0)
     for n in (1, 2, 3):
         got_y(n, 0)
         across(n, 0, 1)
+    project(0, 0)
     got_y(0, 1)
-    unit_to_z(1)
     across(0, 1, 1)
     got_here(0, 2)
     to_z(0, 2)
     to_y(0, 2)
     got_here(0, 2, 1)
+    to_z(0, 2, 1)
     to_y(0, 2, 1)
+    rest_to_z(1)
     for n in (1, 2, 3):
         got_here(n, -1)
         to_y(n, -1)
-    project(1, 1, 2, 3, 4)
     got_y(0, -1)
     across(0, -1, 2)
+    project(1, 1, 2, 3, 4)
     forward(0)
     for n in (1, 2, 3):
         got_here(n, 2)
         to_y(n, 2)
+    project(2, 5)
     got_y(0, 2, 1)
-    unit_to_z(2)
-    project(2, 5)
+    rest_to_z(2)
     got_y(0, 2)
     across(0, 2, 3)
     for n in (1, 2, 3):
-        got_unit(n, 1)
+        got_here(n, 1)
+        got_rest(n, 1)
         across(n, 1, 3)
-    forward(1, 2)
     for n in (1, 2, 3):
         got_y(n, -1)
         across(n, -1, 4)
+    forward(1, 2)
     project(3, 6, 7, 8, 9)
+    project(4, 10, 11, 12)
     forward(3, 4, 5)
     for n in (1, 2, 3):
-        got_unit(n, 2)
+        got_here(n, 2, 1)
+        got_rest(n, 2)
         got_y(n, 2)
         across(n, 2, 5)
-    project(4, 10, 11, 12)
     project(5, 13, 14, 15)
     for m in range(6, 16):
         forward(m)
@@ -339,7 +349,7 @@
         kernel,
         out_shape=jax.ShapeDtypeStruct((SEQ, 512), bf16),
         in_specs=[smem, smem, hbm, hbm, hbm, hbm],
-        out_specs=hbm,
+        out_specs=pl.BlockSpec(memory_space=pl.ANY),
         scratch_shapes=[
             pltpu.VMEM((3, SEQ, FEAT), bf16),
             pltpu.VMEM((SEQ, FEAT), bf16),

time: 58.2 us -> 57 us (0.979)
  the two profiles are of different devices: /device:TPU:4 before, /device:TPU:1 now
where the time goes in v4:
time: 57 us; the launch traced here: 56 us
  Pallas kernels  53.1 us (93%)
  local copies, waits for them, and re-layouts  1.55 us (3%)
  between operations  1.31 us (2%)
    pallas_call x1, Pallas kernels, shards(): pl.pallas_call(kernel, out_shape=jax.ShapeDtypeStruct((SEQ, 512), bf16),...  53.1 us
    unnamed x3, local copies, waits for them, and re-layouts  1.55 us

profile of v4, /device:TPU:1, one launch (start us, length us, event | category | flops | bytes accessed | tf_op | source)
XLA Modules:
  0.0 56.0 jit_solution(1420087804800365632)
XLA Ops:
  1.3 0.0 copy-start
  1.3 0.7 %copy-done = bf16[1024,16]{0,1:T(8,128)(2,1)S(1)} copy-done((bf16[1024,16]{0,1:T(8,128)(2,1)S(1)}, bf16[1024,16]{0,1:T(8,128)(2,1)}, u32[]{:S(2)}) %copy-start) | copy-done | bytes 32792
  2.1 53.1 %attend_project.1 = bf16[512,512]{1,0:T(8,128)(2,1)S(1)} custom-call(s32[1]{0:T(128)S(6)} %copy.8.start_ref, s32[1]{0:T(128)S(6)} %copy.9.len_ref, bf16[512,1024]{1,0:T(8,128)(2,1)} %q_hbm.1, bf16[512,1024]{1,0:T(8,128)(2,1)} %k_hbm.1, bf16[512,1024]{1,0:T(8,128)(2,1)} %v_hbm.1, bf16[16,1024]{1,0:T(8,128)(2,1)S(1)} %bitcast.1), custom_call_target="tpu_custom_call" | custom-call | tf_op jit(solution)/shard_map/attend_project/pallas_call | solution.py:348
  55.2 0.8 %copy.10 = bf16[512,512]{1,0:T(8,128)(2,1)} copy(bf16[512,512]{1,0:T(8,128)(2,1)S(1)} %attend_project.1) | data formatting | bytes 1048576
Async XLA Ops:
  1.3 0.8 %copy-start = (bf16[1024,16]{0,1:T(8,128)(2,1)S(1)}, bf16[1024,16]{0,1:T(8,128)(2,1)}, u32[]{:S(2)}) copy-start(bf16[1024,16]{0,1:T(8,128)(2,1)} %param.9) | copy-start | bytes 98308

commit v5 on v4

--- a/solution.py
+++ b/solution.py
@@ -24,16 +24,20 @@
     cols = pl.ds(pl.multiple_of(h * HD, HD), HD)
     key = k_ref[:, cols]
     val = v_ref[:, cols]
-    for qb in range(SEQ // BLK):
-        rows = pl.ds(qb * BLK, BLK)
-        keys = BLK if qb == 0 else SEQ
-        s = lax.dot_general(q_ref[rows, cols], key[:keys], TRANS, preferred_element_type=jnp.float32)
-        s = s + bias[rows, pl.ds(0, keys)]
+    bounds = ((0, BLK, BLK), (BLK, 2 * BLK, SEQ), (2 * BLK, 3 * BLK, SEQ), (3 * BLK, SEQ, SEQ))
+    scores = []
+    for begin, end, keys in bounds:
+        s = lax.dot_general(q_ref[begin:end, cols], key[:keys], TRANS, preferred_element_type=jnp.float32)
+        scores.append(s + bias[begin:end, :keys])
+    outs = []
+    for s, (begin, end, keys) in zip(scores, bounds):
         top = jnp.max(s, axis=-1, keepdims=True)
         p = jnp.exp2((s - top) * SCALE)
         total = jnp.sum(p, axis=-1, keepdims=True)
         o = jnp.dot(p.astype(jnp.bfloat16), val[:keys], preferred_element_type=jnp.float32)
-        att[rows, cols] = (o / total).astype(jnp.bfloat16)
+        outs.append((o / total).astype(jnp.bfloat16))
+    for o, (begin, end, keys) in zip(outs, bounds):
+        att[begin:end, cols] = o
 
 
 def kernel(start_ref, len_ref, q_hbm, k_hbm, v_hbm, w_hbm, o_hbm,

time: 57 us -> 55.5 us (0.974)
  Pallas kernels: 53.1 us -> 51.7 us
    pallas_call x1, Pallas kernels: 53.1 us -> 51.7 us  [shards(): pl.pallas_call(kernel, out_shape=jax.ShapeDtypeStruct((SEQ, 512), bf16),...]
where the time goes in v5:
time: 55.5 us; the launch traced here: 54.5 us
  Pallas kernels  51.7 us (93%)
  local copies, waits for them, and re-layouts  1.55 us (3%)
  between operations  1.31 us (2%)
    pallas_call x1, Pallas kernels, shards(): pl.pallas_call(kernel, out_shape=jax.ShapeDtypeStruct((SEQ, 512), bf16),...  51.7 us
    unnamed x3, local copies, waits for them, and re-layouts  1.55 us

profile of v5, /device:TPU:1, one launch (start us, length us, event | category | flops | bytes accessed | tf_op | source)
XLA Modules:
  0.0 54.5 jit_solution(16010865954020205195)
XLA Ops:
  1.3 0.0 copy-start
  1.3 0.7 %copy-done = bf16[1024,16]{0,1:T(8,128)(2,1)S(1)} copy-done((bf16[1024,16]{0,1:T(8,128)(2,1)S(1)}, bf16[1024,16]{0,1:T(8,128)(2,1)}, u32[]{:S(2)}) %copy-start) | copy-done | bytes 32792
  2.1 51.7 %attend_project.1 = bf16[512,512]{1,0:T(8,128)(2,1)S(1)} custom-call(s32[1]{0:T(128)S(6)} %copy.8.start_ref, s32[1]{0:T(128)S(6)} %copy.9.len_ref, bf16[512,1024]{1,0:T(8,128)(2,1)} %q_hbm.1, bf16[512,1024]{1,0:T(8,128)(2,1)} %k_hbm.1, bf16[512,1024]{1,0:T(8,128)(2,1)} %v_hbm.1, bf16[16,1024]{1,0:T(8,128)(2,1)S(1)} %bitcast.1), custom_call_target="tpu_custom_call" | custom-call | tf_op jit(solution)/shard_map/attend_project/pallas_call | solution.py:352
  53.7 0.8 %copy.10 = bf16[512,512]{1,0:T(8,128)(2,1)} copy(bf16[512,512]{1,0:T(8,128)(2,1)S(1)} %attend_project.1) | data formatting | bytes 1048576
Async XLA Ops:
  1.3 0.8 %copy-start = (bf16[1024,16]{0,1:T(8,128)(2,1)S(1)}, bf16[1024,16]{0,1:T(8,128)(2,1)}, u32[]{:S(2)}) copy-start(bf16[1024,16]{0,1:T(8,128)(2,1)} %param.9) | copy-start | bytes 98308
